TPU v7x, 32 devices: a whole 2x2x4 slice. The times are simulated.
32 devices in a mesh: dp: 4 (over y, core), blk: 8 (over z, x).
Axes of the slice: x: 2, y: 2, z: 4, core: 2. Of those that a mesh axis runs over, the one named last changes fastest.
Arguments:
- pre_gelu: bfloat16 [6144, 4096], P(('dp', 'blk')), may hold values from -8 to 8
- out_grad: bfloat16 [6144, 1024], P(('dp', 'blk')), may hold values from -6 to 6
- down_weight: bfloat16 [4096, 1024], P('blk'), may hold values from -0.09375 to 0.09375
Outputs:
- block_out: bfloat16 [6144, 1024], P(('dp', 'blk'))
- pre_grad: bfloat16 [6144, 4096], P(('dp', 'blk'))
- weight_grad: float32 [4096, 1024], P('blk')
All inputs are finite; a program needn't handle non-finite values.
Results may differ from a plain program's by a relative error of at most 0.017.
Values may be sent and summed in bfloat16 or wider, within the bound.
No kernel may reach another device: no remote copies, remote signals or barrier semaphores. Data moves between devices by JAX's collectives and lax.ppermute only.
A program may use at most 64 MiB of HBM per device.

v0:
```python
import math
import jax
import jax.numpy as jnp
from jax import lax
from jax.sharding import PartitionSpec as P

SQRT_TWO_PI = 0.7978845608028654
CUBIC = 0.044715


def passed_along(array, axis, by):
    peers = lax.axis_size(axis)
    return lax.ppermute(array, axis, [(i, (i + by) % peers) for i in range(peers)])


def gelu_parts(inputs):
    argument = SQRT_TWO_PI * (inputs + CUBIC * inputs * inputs * inputs)
    tangent = jnp.tanh(argument)
    activation = 0.5 * inputs * (1.0 + tangent)
    derivative = 0.5 * (1.0 + tangent) + 0.5 * inputs * (1.0 - tangent * tangent) * SQRT_TWO_PI * (
        1.0 + 3.0 * CUBIC * inputs * inputs
    )
    return (activation, derivative)


def finish_partial(arrived, own_term):
    rounded = (arrived.astype(jnp.float32) + own_term).astype(jnp.bfloat16)
    return lax.optimization_barrier(rounded).astype(jnp.float32)


def body(pre_gelu, out_grad, down_weight):
    row_count = pre_gelu.shape[0]
    block_rows = down_weight.shape[0]
    cycle_size = lax.axis_size("blk")
    home_index = lax.axis_index("blk")
    activation, derivative = gelu_parts(pre_gelu.astype(jnp.float32))
    hidden = activation.astype(jnp.bfloat16)
    weights_all = lax.all_gather(down_weight, "blk", axis=0, tiled=True)
    out_total = jnp.dot(hidden, weights_all, preferred_element_type=jnp.float32)
    d_hidden = lax.dot_general(
        out_grad, weights_all, (((1,), (1,)), ((), ())), preferred_element_type=jnp.float32
    )
    grad_buffer = (d_hidden * derivative).astype(jnp.bfloat16)

    def block_term(block_index):
        hidden_part = lax.dynamic_slice_in_dim(hidden, block_index * block_rows, block_rows, 1)
        return lax.dot_general(
            hidden_part, out_grad, (((0,), (0,)), ((), ())), preferred_element_type=jnp.float32
        )

    def pass_chain(partial_value):
        return passed_along(partial_value, "blk", 1)

    own_term = block_term(home_index)
    partial_value = block_term(jnp.mod(home_index - 1, cycle_size)).astype(jnp.bfloat16)

    def chain_stop(stop_number, partial_value):
        contribution = block_term(jnp.mod(home_index - stop_number, cycle_size))
        return (pass_chain(partial_value).astype(jnp.float32) + contribution).astype(jnp.bfloat16)

    partial_value = lax.fori_loop(2, cycle_size, chain_stop, partial_value)
    finished = finish_partial(pass_chain(partial_value), own_term)
    summed = lax.psum(finished.astype(jnp.bfloat16), "dp").astype(jnp.float32)
    token_count = row_count * cycle_size * lax.axis_size("dp")
    return (out_total.astype(jnp.bfloat16), grad_buffer, summed / math.sqrt(token_count))


def solution(mesh):
    in_specs = (P(("dp", "blk"), None), P(("dp", "blk"), None), P("blk", None))
    out_specs = (P(("dp", "blk"), None), P(("dp", "blk"), None), P("blk", None))
    return jax.shard_map(body, mesh=mesh, in_specs=in_specs, out_specs=out_specs, check_vma=False)
```

profile of v0, /device:TPU:0, one launch (start us, length us, event | category | flops | bytes accessed | tf_op | source)
XLA Modules:
  0.0 344.3 jit_solution(13820292704655213971)
XLA Ops:
  8.0 0.0 all-reduce.2.cloned.1.call-start
  8.1 2.5 fusion.8
  10.6 1.5 convolution_convert_fusion
  12.1 165.6 %while.15 = (s32[]{:T(128)}, bf16[512,1024]{1,0:T(8,128)(2,1)}, s32[]{:T(128)}, bf16[192,4096]{1,0:T(8,128)(2,1)S(1)}, bf16[192,1024]{1,0:T(8,128)(2,1)S(1)}, /*...) while((s32[]{:T(128)}, bf16[512,1024]{1,0:T(8,128)(2,1)}, ...), condition=%wide.region_1.2_spmd, body=%wide.region_0.1_spmd.sunk | while | flops 202899472 | bytes 6881620 | solution.py:61
  12.1 3.0 collective-permute-start
  15.0 26.4 %collective-permute-done = bf16[512,1024]{1,0:T(8,128)(2,1)S(1)} collective-permute-done((bf16[512,1024]{1,0:T(8,128)(2,1)}, bf16[512,1024]{1,0:T(8,128)(2,1)S(1)}, u32[]{:S(2)}, u32[]{:S(2)}) %collective-permute-start) | collective-permute-done | bytes 1048608 | tf_op jit(solution)/shard_map/while/body/eval_jaxpr/ppermute | solution.py:13
  41.4 1.4 add_convert_fusion.3
  42.9 0.0 collective-permute-start
  42.9 27.2 %collective-permute-done = bf16[512,1024]{1,0:T(8,128)(2,1)S(1)} collective-permute-done((bf16[512,1024]{1,0:T(8,128)(2,1)}, bf16[512,1024]{1,0:T(8,128)(2,1)S(1)}, u32[]{:S(2)}, u32[]{:S(2)}) %collective-permute-start) | collective-permute-done | bytes 1048608 | tf_op jit(solution)/shard_map/while/body/eval_jaxpr/ppermute | solution.py:13
  70.1 1.4 add_convert_fusion.3
  71.6 0.0 collective-permute-start
  71.6 26.4 %collective-permute-done = bf16[512,1024]{1,0:T(8,128)(2,1)S(1)} collective-permute-done((bf16[512,1024]{1,0:T(8,128)(2,1)}, bf16[512,1024]{1,0:T(8,128)(2,1)S(1)}, u32[]{:S(2)}, u32[]{:S(2)}) %collective-permute-start) | collective-permute-done | bytes 1048608 | tf_op jit(solution)/shard_map/while/body/eval_jaxpr/ppermute | solution.py:13
  97.9 1.4 add_convert_fusion.3
  99.4 0.0 collective-permute-start
  99.4 25.5 %collective-permute-done = bf16[512,1024]{1,0:T(8,128)(2,1)S(1)} collective-permute-done((bf16[512,1024]{1,0:T(8,128)(2,1)}, bf16[512,1024]{1,0:T(8,128)(2,1)S(1)}, u32[]{:S(2)}, u32[]{:S(2)}) %collective-permute-start) | collective-permute-done | bytes 1048608 | tf_op jit(solution)/shard_map/while/body/eval_jaxpr/ppermute | solution.py:13
  124.9 1.4 add_convert_fusion.3
  126.3 24.7 %collective-permute-done = bf16[512,1024]{1,0:T(8,128)(2,1)S(1)} collective-permute-done((bf16[512,1024]{1,0:T(8,128)(2,1)}, bf16[512,1024]{1,0:T(8,128)(2,1)S(1)}, u32[]{:S(2)}, u32[]{:S(2)}) %collective-permute-start) | collective-permute-done | bytes 1048608 | tf_op jit(solution)/shard_map/while/body/eval_jaxpr/ppermute | solution.py:13
  151.0 1.4 add_convert_fusion.3
  152.4 0.0 collective-permute-start
  152.4 23.8 %collective-permute-done = bf16[512,1024]{1,0:T(8,128)(2,1)S(1)} collective-permute-done((bf16[512,1024]{1,0:T(8,128)(2,1)}, bf16[512,1024]{1,0:T(8,128)(2,1)S(1)}, u32[]{:S(2)}, u32[]{:S(2)}) %collective-permute-start) | collective-permute-done | bytes 1048608 | tf_op jit(solution)/shard_map/while/body/eval_jaxpr/ppermute | solution.py:13
  176.3 1.4 add_convert_fusion.3
  177.7 0.0 collective-permute-start.1
  177.7 23.0 %collective-permute-done.1 = bf16[512,1024]{1,0:T(8,128)(2,1)S(1)} collective-permute-done((bf16[512,1024]{1,0:T(8,128)(2,1)}, bf16[512,1024]{1,0:T(8,128)(2,1)S(1)}, u32[]{:S(2)}, u32[]{:S(2)}) %collective-permute-start.1) | collective-permute-done | bytes 1048608 | tf_op jit(solution)/shard_map/ppermute | solution.py:13
  200.7 1.4 add_convert_fusion.1
  202.1 0.0 all-reduce.2.cloned.1.call-update
  202.1 0.0 all-gather.2.cloned.1.call-start
  202.2 0.5 all-gather.2.cloned.1.call-update
  202.7 32.3 %all-reduce.2.cloned.1.call-done = bf16[512,1024]{1,0:T(8,128)(2,1)} async-done(((bf16[512,1024]{1,0:T(8,128)(2,1)}), bf16[512,1024]{1,0:T(8,128)(2,1)}) %all-reduce.2.cloned.1.call-update) | async-done | bytes 1048592 | tf_op jit(solution)/shard_map/psum | solution.py:63
  235.0 2.8 convert_multiply_fusion.6
  237.8 87.2 %all-gather.2.cloned.1.call-done = bf16[4096,1024]{1,0:T(8,128)(2,1)} async-done(((bf16[512,1024]{1,0:T(8,128)(2,1)}), bf16[4096,1024]{1,0:T(8,128)(2,1)}) %all-gather.2.cloned.1.call-update) | async-done | bytes 8388624 | tf_op jit(solution)/shard_map/all_gather | solution.py:38
  325.0 6.5 %convolution_convert_fusion.1 = bf16[192,1024]{1,0:T(8,128)(2,1)} fusion(bf16[4096,1024]{1,0:T(8,128)(2,1)} %all-gather.2.cloned.1.call-done, bf16[192,4096]{1,0:T(8,128)(2,1)S(1)} %copy-done.1), kind=kOutput, calls=%fused_computation.25 | convolution fusion | flops 1618673664 | bytes 10354688 | tf_op jit(solution)/shard_map/dot_general | solution.py:39
  331.5 5.3 %fusion.5 = bf16[192,4096]{1,0:T(8,128)(2,1)} fusion(bf16[192,1024]{1,0:T(8,128)(2,1)S(1)} %get-tuple-element.217, bf16[4096,1024]{1,0:T(8,128)(2,1)S(1)} %copy-done.2, bf16[192,4096]{1,0:T(8,128)(2,1)S(1)} %copy-done.1), kind=kOutput, calls=%fused_computation.12 | convolution fusion | flops 1626341376 | bytes 11927552 | tf_op jit(solution)/shard_map/dot_general | solution.py:40
  (7 shorter events, 0.0 us)
Async XLA Ops:
  8.0 2.6 copy-start
  8.0 227.0 %all-reduce.2.cloned.1.call-start = ((), (), s32[]{:S(2)}) async-start(), calls=%async_computation.1 | async-start | bytes 2097152 | tf_op jit(solution)/shard_map/psum | solution.py:63
  12.1 29.4 %collective-permute-start = (bf16[512,1024]{1,0:T(8,128)(2,1)}, bf16[512,1024]{1,0:T(8,128)(2,1)S(1)}, u32[]{:S(2)}, u32[]{:S(2)}) collective-permute-start(bf16[512,1024]{1,0:T(8,128)(2,1)} %get-tuple-element.191), channel_id=1, source_target_pairs={{0,1},{1,2},{2,3},{3,4},{4,5},{5,6},{6,7},{7,0},{8,9},{9,10},{10,1... | collective-permute-start | bytes 3145736 | tf_op jit(solution)/shard_map/while/body/eval_jaxpr/ppermute | solution.py:13
  42.9 27.2 %collective-permute-start = (bf16[512,1024]{1,0:T(8,128)(2,1)}, bf16[512,1024]{1,0:T(8,128)(2,1)S(1)}, u32[]{:S(2)}, u32[]{:S(2)}) collective-permute-start(bf16[512,1024]{1,0:T(8,128)(2,1)} %get-tuple-element.191), channel_id=1, source_target_pairs={{0,1},{1,2},{2,3},{3,4},{4,5},{5,6},{6,7},{7,0},{8,9},{9,10},{10,1... | collective-permute-start | bytes 3145736 | tf_op jit(solution)/shard_map/while/body/eval_jaxpr/ppermute | solution.py:13
  71.6 26.4 %collective-permute-start = (bf16[512,1024]{1,0:T(8,128)(2,1)}, bf16[512,1024]{1,0:T(8,128)(2,1)S(1)}, u32[]{:S(2)}, u32[]{:S(2)}) collective-permute-start(bf16[512,1024]{1,0:T(8,128)(2,1)} %get-tuple-element.191), channel_id=1, source_target_pairs={{0,1},{1,2},{2,3},{3,4},{4,5},{5,6},{6,7},{7,0},{8,9},{9,10},{10,1... | collective-permute-start | bytes 3145736 | tf_op jit(solution)/shard_map/while/body/eval_jaxpr/ppermute | solution.py:13
  99.4 25.5 %collective-permute-start = (bf16[512,1024]{1,0:T(8,128)(2,1)}, bf16[512,1024]{1,0:T(8,128)(2,1)S(1)}, u32[]{:S(2)}, u32[]{:S(2)}) collective-permute-start(bf16[512,1024]{1,0:T(8,128)(2,1)} %get-tuple-element.191), channel_id=1, source_target_pairs={{0,1},{1,2},{2,3},{3,4},{4,5},{5,6},{6,7},{7,0},{8,9},{9,10},{10,1... | collective-permute-start | bytes 3145736 | tf_op jit(solution)/shard_map/while/body/eval_jaxpr/ppermute | solution.py:13
  126.3 24.7 %collective-permute-start = (bf16[512,1024]{1,0:T(8,128)(2,1)}, bf16[512,1024]{1,0:T(8,128)(2,1)S(1)}, u32[]{:S(2)}, u32[]{:S(2)}) collective-permute-start(bf16[512,1024]{1,0:T(8,128)(2,1)} %get-tuple-element.191), channel_id=1, source_target_pairs={{0,1},{1,2},{2,3},{3,4},{4,5},{5,6},{6,7},{7,0},{8,9},{9,10},{10,1... | collective-permute-start | bytes 3145736 | tf_op jit(solution)/shard_map/while/body/eval_jaxpr/ppermute | solution.py:13
  152.4 23.8 %collective-permute-start = (bf16[512,1024]{1,0:T(8,128)(2,1)}, bf16[512,1024]{1,0:T(8,128)(2,1)S(1)}, u32[]{:S(2)}, u32[]{:S(2)}) collective-permute-start(bf16[512,1024]{1,0:T(8,128)(2,1)} %get-tuple-element.191), channel_id=1, source_target_pairs={{0,1},{1,2},{2,3},{3,4},{4,5},{5,6},{6,7},{7,0},{8,9},{9,10},{10,1... | collective-permute-start | bytes 3145736 | tf_op jit(solution)/shard_map/while/body/eval_jaxpr/ppermute | solution.py:13
  177.7 23.0 %collective-permute-start.1 = (bf16[512,1024]{1,0:T(8,128)(2,1)}, bf16[512,1024]{1,0:T(8,128)(2,1)S(1)}, u32[]{:S(2)}, u32[]{:S(2)}) collective-permute-start(bf16[512,1024]{1,0:T(8,128)(2,1)} %get-tuple-element.136), channel_id=1, source_target_pairs={{0,1},{1,2},{2,3},{3,4},{4,5},{5,6},{6,7},{7,0},{8,9},{9,10},{10,1... | collective-permute-start | bytes 3145736 | tf_op jit(solution)/shard_map/ppermute | solution.py:13
  202.1 122.9 %copy-start.1 = (bf16[192,4096]{1,0:T(8,128)(2,1)S(1)}, bf16[192,4096]{1,0:T(8,128)(2,1)}, u32[]{:S(2)}) copy-start(bf16[192,4096]{1,0:T(8,128)(2,1)} %param.5) | copy-start | bytes 4718596
  202.1 122.9 %all-gather.2.cloned.1.call-start = ((), (), s32[]{:S(2)}) async-start(), calls=%async_computation | async-start | bytes 9437184 | tf_op jit(solution)/shard_map/all_gather | solution.py:38
  325.0 6.5 %copy-start.2 = (bf16[4096,1024]{1,0:T(8,128)(2,1)S(1)}, bf16[4096,1024]{1,0:T(8,128)(2,1)}, u32[]{:S(2)}) copy-start(bf16[4096,1024]{1,0:T(8,128)(2,1)} %all-gather.2.cloned.1.call-done) | copy-start | bytes 25165828
Sparse Core Ops, SparseCore 0:
  202.2 32.6 all-reduce.1
Sparse Core Ops, SparseCore 1:
  204.7 120.2 all-gather.1
where the time goes:
time: 344 us
  waiting for transfers between devices  297 us (86%)
  matrix products  23.3 us (7%)
  between operations  15.5 us (5%)
  other arithmetic  5.35 us (2%)
    ppermute x7, waiting for transfers between devices, passed_along(): lax.ppermute(array, axis, [(i, (i + by) % peers) for i in range(peers)])  177 us
    all_gather x1, waiting for transfers between devices, body(): weights_all = lax.all_gather(down_weight, 'blk', axis=0, tiled=True)  87.2 us
    psum x1, waiting for transfers between devices, body(): summed = lax.psum(finished.astype(jnp.bfloat16), 'dp').astype(jnp.float32)  32.3 us
    dot_general x8, matrix products, block_term(): lax.dot_general(hidden_part, out_grad, (((0,), (0,)), ((), ())), preferre...  11.6 us
  transfers between devices with their start and end apart: 9, of which 9 were waited for; matrix products, arithmetic and copies ran while one was open for 1% of the time, Pallas kernels for 0%

commit v1 on v0

--- a/solution.py
+++ b/solution.py
@@ -60,7 +60,9 @@
 
     partial_value = lax.fori_loop(2, cycle_size, chain_stop, partial_value)
     finished = finish_partial(pass_chain(partial_value), own_term)
-    summed = lax.psum(finished.astype(jnp.bfloat16), "dp").astype(jnp.float32)
+    summed = jnp.sum(lax.all_gather(finished.astype(jnp.bfloat16), "dp"), axis=0).astype(
+        jnp.float32
+    )
     token_count = row_count * cycle_size * lax.axis_size("dp")
     return (out_total.astype(jnp.bfloat16), grad_buffer, summed / math.sqrt(token_count))
 

time: 344 us -> 377 us (1.096)
  waiting for transfers between devices: 297 us -> 329 us
    all_gather x1, waiting for transfers between devices: 87.2 us -> 122 us  [body(): weights_all = lax.all_gather(down_weight, 'blk', axis=0, tiled=True)]
    psum x1 -> x0, waiting for transfers between devices: 32.3 us -> none  [body(): summed = lax.psum(finished.astype(jnp.bfloat16), 'dp').astype(jnp.float32)]
    all_gather x0 -> x1, waiting for transfers between devices: none -> 30 us  [body(): lax.all_gather(finished.astype(jnp.bfloat16), 'dp')]
where the time goes in v1:
time: 377 us
  waiting for transfers between devices  329 us (87%)
  matrix products  23.3 us (6%)
  between operations  14.1 us (4%)
  other arithmetic  7.56 us (2%)
    ppermute x7, waiting for transfers between devices, passed_along(): lax.ppermute(array, axis, [(i, (i + by) % peers) for i in range(peers)])  177 us
    all_gather x1, waiting for transfers between devices, body(): weights_all = lax.all_gather(down_weight, 'blk', axis=0, tiled=True)  122 us
    all_gather x1, waiting for transfers between devices, body(): lax.all_gather(finished.astype(jnp.bfloat16), 'dp')  30 us
    dot_general x8, matrix products, block_term(): lax.dot_general(hidden_part, out_grad, (((0,), (0,)), ((), ())), preferre...  11.6 us
  transfers between devices with their start and end apart: 9, of which 9 were waited for; matrix products, arithmetic and copies ran while one was open for 1% of the time, Pallas kernels for 0%

profile of v1, /device:TPU:0, one launch (start us, length us, event | category | flops | bytes accessed | tf_op | source)
XLA Modules:
  0.0 377.3 jit_solution(7196080881786498649)
XLA Ops:
  7.2 0.0 all-gather.6.cloned.1.call-start
  7.2 2.5 fusion.8
  9.8 1.5 convolution_convert_fusion
  11.2 165.6 %while.15 = (s32[]{:T(128)}, bf16[512,1024]{1,0:T(8,128)(2,1)}, s32[]{:T(128)}, bf16[192,4096]{1,0:T(8,128)(2,1)S(1)}, bf16[192,1024]{1,0:T(8,128)(2,1)S(1)}, /*...) while((s32[]{:T(128)}, bf16[512,1024]{1,0:T(8,128)(2,1)}, ...), condition=%wide.region_1.2_spmd, body=%wide.region_0.1_spmd.sunk | while | flops 202899472 | bytes 6881620 | solution.py:61
  11.2 3.0 collective-permute-start
  14.2 26.4 %collective-permute-done = bf16[512,1024]{1,0:T(8,128)(2,1)S(1)} collective-permute-done((bf16[512,1024]{1,0:T(8,128)(2,1)}, bf16[512,1024]{1,0:T(8,128)(2,1)S(1)}, u32[]{:S(2)}, u32[]{:S(2)}) %collective-permute-start) | collective-permute-done | bytes 1048608 | tf_op jit(solution)/shard_map/while/body/eval_jaxpr/ppermute | solution.py:13
  40.6 1.4 add_convert_fusion.3
  42.0 0.0 collective-permute-start
  42.0 27.2 %collective-permute-done = bf16[512,1024]{1,0:T(8,128)(2,1)S(1)} collective-permute-done((bf16[512,1024]{1,0:T(8,128)(2,1)}, bf16[512,1024]{1,0:T(8,128)(2,1)S(1)}, u32[]{:S(2)}, u32[]{:S(2)}) %collective-permute-start) | collective-permute-done | bytes 1048608 | tf_op jit(solution)/shard_map/while/body/eval_jaxpr/ppermute | solution.py:13
  69.3 1.4 add_convert_fusion.3
  70.7 0.0 collective-permute-start
  70.7 26.4 %collective-permute-done = bf16[512,1024]{1,0:T(8,128)(2,1)S(1)} collective-permute-done((bf16[512,1024]{1,0:T(8,128)(2,1)}, bf16[512,1024]{1,0:T(8,128)(2,1)S(1)}, u32[]{:S(2)}, u32[]{:S(2)}) %collective-permute-start) | collective-permute-done | bytes 1048608 | tf_op jit(solution)/shard_map/while/body/eval_jaxpr/ppermute | solution.py:13
  97.1 1.4 add_convert_fusion.3
  98.6 25.5 %collective-permute-done = bf16[512,1024]{1,0:T(8,128)(2,1)S(1)} collective-permute-done((bf16[512,1024]{1,0:T(8,128)(2,1)}, bf16[512,1024]{1,0:T(8,128)(2,1)S(1)}, u32[]{:S(2)}, u32[]{:S(2)}) %collective-permute-start) | collective-permute-done | bytes 1048608 | tf_op jit(solution)/shard_map/while/body/eval_jaxpr/ppermute | solution.py:13
  124.1 1.4 add_convert_fusion.3
  125.5 24.7 %collective-permute-done = bf16[512,1024]{1,0:T(8,128)(2,1)S(1)} collective-permute-done((bf16[512,1024]{1,0:T(8,128)(2,1)}, bf16[512,1024]{1,0:T(8,128)(2,1)S(1)}, u32[]{:S(2)}, u32[]{:S(2)}) %collective-permute-start) | collective-permute-done | bytes 1048608 | tf_op jit(solution)/shard_map/while/body/eval_jaxpr/ppermute | solution.py:13
  150.2 1.4 add_convert_fusion.3
  151.6 0.0 collective-permute-start
  151.6 23.8 %collective-permute-done = bf16[512,1024]{1,0:T(8,128)(2,1)S(1)} collective-permute-done((bf16[512,1024]{1,0:T(8,128)(2,1)}, bf16[512,1024]{1,0:T(8,128)(2,1)S(1)}, u32[]{:S(2)}, u32[]{:S(2)}) %collective-permute-start) | collective-permute-done | bytes 1048608 | tf_op jit(solution)/shard_map/while/body/eval_jaxpr/ppermute | solution.py:13
  175.4 1.4 add_convert_fusion.3
  176.9 0.0 collective-permute-start.1
  176.9 22.9 %collective-permute-done.1 = bf16[512,1024]{1,0:T(8,128)(2,1)S(1)} collective-permute-done((bf16[512,1024]{1,0:T(8,128)(2,1)}, bf16[512,1024]{1,0:T(8,128)(2,1)S(1)}, u32[]{:S(2)}, u32[]{:S(2)}) %collective-permute-start.1) | collective-permute-done | bytes 1048608 | tf_op jit(solution)/shard_map/ppermute | solution.py:13
  199.8 1.4 add_convert_fusion.1
  201.2 0.0 all-gather.6.cloned.1.call-update
  201.3 0.0 all-gather.4.cloned.1.call-start
  201.3 0.7 all-gather.4.cloned.1.call-update
  202.0 30.0 %all-gather.6.cloned.1.call-done = bf16[2048,1024]{1,0:T(8,128)(2,1)} async-done(((bf16[512,1024]{1,0:T(8,128)(2,1)}), bf16[2048,1024]{1,0:T(8,128)(2,1)}) %all-gather.6.cloned.1.call-update) | async-done | bytes 4194320 | tf_op jit(solution)/shard_map/all_gather | solution.py:63
  232.0 3.4 reduce_sum.12
  235.5 1.6 convert_multiply_fusion.6
  237.1 121.6 %all-gather.4.cloned.1.call-done = bf16[4096,1024]{1,0:T(8,128)(2,1)} async-done(((bf16[512,1024]{1,0:T(8,128)(2,1)}), bf16[4096,1024]{1,0:T(8,128)(2,1)}) %all-gather.4.cloned.1.call-update) | async-done | bytes 8388624 | tf_op jit(solution)/shard_map/all_gather | solution.py:38
  358.6 6.5 %convolution_convert_fusion.1 = bf16[192,1024]{1,0:T(8,128)(2,1)} fusion(bf16[4096,1024]{1,0:T(8,128)(2,1)} %all-gather.4.cloned.1.call-done, bf16[192,4096]{1,0:T(8,128)(2,1)S(1)} %copy-done.1), kind=kOutput, calls=%fused_computation.25 | convolution fusion | flops 1618673664 | bytes 10354688 | tf_op jit(solution)/shard_map/dot_general | solution.py:39
  365.1 5.3 %fusion.5 = bf16[192,4096]{1,0:T(8,128)(2,1)} fusion(bf16[192,1024]{1,0:T(8,128)(2,1)S(1)} %get-tuple-element.217, bf16[4096,1024]{1,0:T(8,128)(2,1)S(1)} %copy-done.2, bf16[192,4096]{1,0:T(8,128)(2,1)S(1)} %copy-done.1), kind=kOutput, calls=%fused_computation.12 | convolution fusion | flops 1626341376 | bytes 11927552 | tf_op jit(solution)/shard_map/dot_general | solution.py:40
  (8 shorter events, 0.0 us)
Async XLA Ops:
  7.2 2.6 copy-start
  7.2 224.8 %all-gather.6.cloned.1.call-start = ((), (), s32[]{:S(2)}) async-start(), calls=%async_computation.1 | async-start | bytes 5242880 | tf_op jit(solution)/shard_map/all_gather | solution.py:63
  11.2 29.4 %collective-permute-start = (bf16[512,1024]{1,0:T(8,128)(2,1)}, bf16[512,1024]{1,0:T(8,128)(2,1)S(1)}, u32[]{:S(2)}, u32[]{:S(2)}) collective-permute-start(bf16[512,1024]{1,0:T(8,128)(2,1)} %get-tuple-element.191), channel_id=1, source_target_pairs={{0,1},{1,2},{2,3},{3,4},{4,5},{5,6},{6,7},{7,0},{8,9},{9,10},{10,1... | collective-permute-start | bytes 3145736 | tf_op jit(solution)/shard_map/while/body/eval_jaxpr/ppermute | solution.py:13
  42.0 27.2 %collective-permute-start = (bf16[512,1024]{1,0:T(8,128)(2,1)}, bf16[512,1024]{1,0:T(8,128)(2,1)S(1)}, u32[]{:S(2)}, u32[]{:S(2)}) collective-permute-start(bf16[512,1024]{1,0:T(8,128)(2,1)} %get-tuple-element.191), channel_id=1, source_target_pairs={{0,1},{1,2},{2,3},{3,4},{4,5},{5,6},{6,7},{7,0},{8,9},{9,10},{10,1... | collective-permute-start | bytes 3145736 | tf_op jit(solution)/shard_map/while/body/eval_jaxpr/ppermute | solution.py:13
  70.7 26.4 %collective-permute-start = (bf16[512,1024]{1,0:T(8,128)(2,1)}, bf16[512,1024]{1,0:T(8,128)(2,1)S(1)}, u32[]{:S(2)}, u32[]{:S(2)}) collective-permute-start(bf16[512,1024]{1,0:T(8,128)(2,1)} %get-tuple-element.191), channel_id=1, source_target_pairs={{0,1},{1,2},{2,3},{3,4},{4,5},{5,6},{6,7},{7,0},{8,9},{9,10},{10,1... | collective-permute-start | bytes 3145736 | tf_op jit(solution)/shard_map/while/body/eval_jaxpr/ppermute | solution.py:13
  98.6 25.5 %collective-permute-start = (bf16[512,1024]{1,0:T(8,128)(2,1)}, bf16[512,1024]{1,0:T(8,128)(2,1)S(1)}, u32[]{:S(2)}, u32[]{:S(2)}) collective-permute-start(bf16[512,1024]{1,0:T(8,128)(2,1)} %get-tuple-element.191), channel_id=1, source_target_pairs={{0,1},{1,2},{2,3},{3,4},{4,5},{5,6},{6,7},{7,0},{8,9},{9,10},{10,1... | collective-permute-start | bytes 3145736 | tf_op jit(solution)/shard_map/while/body/eval_jaxpr/ppermute | solution.py:13
  125.5 24.7 %collective-permute-start = (bf16[512,1024]{1,0:T(8,128)(2,1)}, bf16[512,1024]{1,0:T(8,128)(2,1)S(1)}, u32[]{:S(2)}, u32[]{:S(2)}) collective-permute-start(bf16[512,1024]{1,0:T(8,128)(2,1)} %get-tuple-element.191), channel_id=1, source_target_pairs={{0,1},{1,2},{2,3},{3,4},{4,5},{5,6},{6,7},{7,0},{8,9},{9,10},{10,1... | collective-permute-start | bytes 3145736 | tf_op jit(solution)/shard_map/while/body/eval_jaxpr/ppermute | solution.py:13
  151.6 23.8 %collective-permute-start = (bf16[512,1024]{1,0:T(8,128)(2,1)}, bf16[512,1024]{1,0:T(8,128)(2,1)S(1)}, u32[]{:S(2)}, u32[]{:S(2)}) collective-permute-start(bf16[512,1024]{1,0:T(8,128)(2,1)} %get-tuple-element.191), channel_id=1, source_target_pairs={{0,1},{1,2},{2,3},{3,4},{4,5},{5,6},{6,7},{7,0},{8,9},{9,10},{10,1... | collective-permute-start | bytes 3145736 | tf_op jit(solution)/shard_map/while/body/eval_jaxpr/ppermute | solution.py:13
  176.9 22.9 %collective-permute-start.1 = (bf16[512,1024]{1,0:T(8,128)(2,1)}, bf16[512,1024]{1,0:T(8,128)(2,1)S(1)}, u32[]{:S(2)}, u32[]{:S(2)}) collective-permute-start(bf16[512,1024]{1,0:T(8,128)(2,1)} %get-tuple-element.136), channel_id=1, source_target_pairs={{0,1},{1,2},{2,3},{3,4},{4,5},{5,6},{6,7},{7,0},{8,9},{9,10},{10,1... | collective-permute-start | bytes 3145736 | tf_op jit(solution)/shard_map/ppermute | solution.py:13
  201.3 157.4 %all-gather.4.cloned.1.call-start = ((), (), s32[]{:S(2)}) async-start(), calls=%async_computation | async-start | bytes 9437184 | tf_op jit(solution)/shard_map/all_gather | solution.py:38
  232.0 126.6 %copy-start.1 = (bf16[192,4096]{1,0:T(8,128)(2,1)S(1)}, bf16[192,4096]{1,0:T(8,128)(2,1)}, u32[]{:S(2)}) copy-start(bf16[192,4096]{1,0:T(8,128)(2,1)} %param.5) | copy-start | bytes 4718596
  358.6 6.5 %copy-start.2 = (bf16[4096,1024]{1,0:T(8,128)(2,1)S(1)}, bf16[4096,1024]{1,0:T(8,128)(2,1)}, u32[]{:S(2)}) copy-start(bf16[4096,1024]{1,0:T(8,128)(2,1)} %all-gather.4.cloned.1.call-done) | copy-start | bytes 25165828
Sparse Core Ops, SparseCore 0:
  201.4 30.5 all-gather.5
  234.1 124.4 all-gather.3
